TPU v7x, 256 devices: a whole 4x4x8 slice. The times are simulated.
256 devices in a mesh: seq: 64 (over z, x, core), head: 4 (over y).
Axes of the slice: x: 4, y: 4, z: 8, core: 2. Of those that a mesh axis runs over, the one named last changes fastest.
Arguments:
- queries: bfloat16 [2048, 2560], P('seq', 'head'), may hold values from -24 to 24
- new_keys: bfloat16 [2048, 2560], P('seq', 'head'), may hold values from -7 to 7
- new_values: bfloat16 [2048, 2560], P('seq', 'head'), may hold values from -6 to 6
- key_cache: bfloat16 [8192, 2560], P('seq', 'head'), may hold values from -7 to 7
- value_cache: bfloat16 [8192, 2560], P('seq', 'head'), may hold values from -6 to 6
- out_weight: bfloat16 [2560, 5120], P('head'), may hold values from -0.125 to 0.125
- gate: float32 [5120], P('head'), may hold values from 0.4 to 1.6
- refresh_index: int32 [64, 32], P('seq'), may hold values from 0 to 127, as said below
- refresh_count: int32 [64], P('seq'), may hold values from 1 to 32, 1024 in all
Outputs:
- update: bfloat16 [2048, 5120], P('seq', 'head')
Inputs may be any that keep to these rules, and one draw needn't show every extreme that they name: `refresh_index`: each row holds 32 distinct token positions of that seq index; only the first refresh_count of them are used. `refresh_count`: the counts sum to 16 times the number of seq indices.
All inputs are finite; a program needn't handle non-finite values. No bound on the sum of `refresh_count` on one device may be relied on, other than what follows from the above.
Results may differ from a plain program's by a relative error of at most 0.015.
Values may be sent and summed in bfloat16 or wider, within the bound.
A program may use at most 64 MiB of HBM per device.

v0:
```python
import jax
import jax.numpy as jnp
from jax import lax
from jax.sharding import PartitionSpec as P

HD = 128


def block_rows():
    return 512


def score_block(q_block, keys_heads, key_scale):
    row_count = q_block.shape[0]
    split = q_block.reshape(row_count, keys_heads.shape[1], keys_heads.shape[2])
    return (
        jnp.einsum("bhd,thd->bht", split, keys_heads, preferred_element_type=jnp.float32)
        * key_scale
    )


def local_top(rows_all, keys_heads, key_scale):
    row_total = rows_all.shape[0]
    per_block = block_rows()
    blocks = rows_all.reshape(row_total // per_block, per_block, rows_all.shape[1])
    row_tops = lax.map(
        lambda q_block: jnp.max(score_block(q_block, keys_heads, key_scale), axis=-1), blocks
    )
    return row_tops.reshape(row_total, keys_heads.shape[1])


def local_sums(rows_all, row_peak, keys_heads, values_heads, key_scale):
    row_total = rows_all.shape[0]
    head_count = keys_heads.shape[1]
    per_block = block_rows()
    blocks = rows_all.reshape(row_total // per_block, per_block, rows_all.shape[1])
    peaks = row_peak.reshape(row_total // per_block, per_block, head_count)

    def per_step(inputs):
        q_block, peak_block = inputs
        weights = jnp.exp(score_block(q_block, keys_heads, key_scale) - peak_block[:, :, None])
        weight_total = jnp.sum(weights, axis=-1)
        summed = jnp.einsum(
            "bht,thd->bhd",
            weights.astype(jnp.bfloat16),
            values_heads,
            preferred_element_type=jnp.float32,
        )
        return (summed.reshape(q_block.shape[0], -1), weight_total)

    summed, totals = lax.map(per_step, (blocks, peaks))
    return (summed.reshape(row_total, -1), totals.reshape(row_total, head_count))


def normalize(summed, totals):
    row_count = summed.shape[0]
    head_count = totals.shape[1]
    shaped = summed.reshape(row_count, head_count, -1) / totals[:, :, None]
    return shaped.reshape(row_count, -1).astype(jnp.bfloat16)


def patch_rows(cache, fresh, index_row, live_slots):
    token_count = cache.shape[0]
    matches = (jnp.arange(token_count)[:, None] == index_row[None, :]) & live_slots[None, :]
    replaced = jnp.any(matches, axis=1)
    placed = jnp.dot(
        matches.astype(jnp.bfloat16), fresh, preferred_element_type=jnp.float32
    ).astype(jnp.bfloat16)
    return jnp.where(replaced[:, None], placed, cache)


def on_device(
    queries,
    new_keys,
    new_values,
    key_cache,
    value_cache,
    out_weight,
    gate,
    refresh_index,
    refresh_count,
):
    slot_count = queries.shape[0]
    row_width = queries.shape[1]
    head_count = row_width // HD
    key_scale = HD ** (-0.5)
    my_count = refresh_count[0]
    live_slots = jnp.arange(slot_count) < my_count
    keys = patch_rows(key_cache, new_keys, refresh_index[0], live_slots)
    values = patch_rows(value_cache, new_values, refresh_index[0], live_slots)
    keys_heads = keys.reshape(keys.shape[0], head_count, HD)
    values_heads = values.reshape(values.shape[0], head_count, HD)
    rows_all = lax.all_gather(queries, "seq", axis=0, tiled=True)
    row_tops = local_top(rows_all, keys_heads, key_scale)
    row_peak = lax.pmax(row_tops.astype(jnp.bfloat16), "seq").astype(row_tops.dtype)
    summed, totals = local_sums(rows_all, row_peak, keys_heads, values_heads, key_scale)
    own_summed, own_totals = (
        lax.psum_scatter(summed, "seq", scatter_dimension=0, tiled=True),
        lax.psum_scatter(totals, "seq", scatter_dimension=0, tiled=True),
    )
    attended = normalize(own_summed, own_totals)
    partial_rows = jnp.dot(attended, out_weight, preferred_element_type=jnp.float32)
    projected = lax.psum_scatter(
        partial_rows.astype(jnp.bfloat16), "head", scatter_dimension=1, tiled=True
    ).astype(jnp.float32)
    live_rows = live_slots.astype(jnp.float32)[:, None]
    return (gate[None, :] * projected * live_rows).astype(jnp.bfloat16)


def solution(mesh):
    return jax.shard_map(
        on_device,
        mesh=mesh,
        in_specs=(
            P("seq", "head"),
            P("seq", "head"),
            P("seq", "head"),
            P("seq", "head"),
            P("seq", "head"),
            P("head", None),
            P("head"),
            P("seq", None),
            P("seq"),
        ),
        out_specs=P("seq", "head"),
        check_vma=False,
    )
```

profile of v0, /device:TPU:1, one launch (start us, length us, event | category | flops | bytes accessed | tf_op | source)
XLA Modules:
  0.0 684.4 jit_solution(10780286917541324576)
XLA Ops:
  6.5 0.7 all-gather.2.cloned.1.call-update
  8.0 0.7 fusion.13
  8.7 1.3 fusion.7
  10.2 1.3 fusion.6
  11.8 80.3 %all-gather.2.cloned.1.call-done = bf16[2048,640]{1,0:T(8,128)(2,1)} async-done(((bf16[32,640]{1,0:T(8,128)(2,1)}), bf16[2048,640]{1,0:T(8,128)(2,1)}) %all-gather.2.cloned.1.call-update) | async-done | bytes 2621456 | tf_op jit(solution)/shard_map/all_gather | solution.py:93
  92.1 4.4 copy.53
  96.5 6.0 while.24
  96.5 1.1 constant_dynamic-slice_fusion.6
  98.0 1.1 constant_dynamic-slice_fusion.6
  99.5 1.1 constant_dynamic-slice_fusion.6
  101.0 1.1 constant_dynamic-slice_fusion.6
  102.5 243.3 %pmax.7 = bf16[4,512,5]{1,2,0:T(8,128)(2,1)S(1)} all-reduce(bf16[4,512,5]{1,2,0:T(8,128)(2,1)S(1)} %get-tuple-element.65), channel_id=1, replica_groups=mesh['seq'=64,'head'=4] {'seq'}, use_global_device_ids=true, to_apply=%region_4.5 | all-reduce | flops 10240 | bytes 40960 | tf_op jit(solution)/shard_map/pmax | solution.py:95
  345.8 13.9 %while.25 = (s32[]{:T(128)}, f32[4,512,640]{2,1,0:T(8,128)}, f32[4,512,5]{1,2,0:T(8,128)S(1)}, bf16[4,512,640]{1,2,0:T(8,128)(2,1)}, bf16[128,5,128]{2,0,1:T(8,1...) while((s32[]{:T(128)}, f32[4,512,640]{2,1,0:T(8,128)}, ...), condition=%wide.region_7.8_spmd.clone, body=%wide.region_5.7_spmd.sunk.clone | while | flops 169080320 | bytes 10231909 | solution.py:51
  345.8 1.1 constant_dynamic-slice_fusion.7
  346.9 0.4 fusion.54
  348.1 1.2 constant_dynamic-update-slice_fusion.3
  349.2 1.1 constant_dynamic-slice_fusion.7
  350.4 0.4 fusion.54
  351.5 1.2 constant_dynamic-update-slice_fusion.3
  352.7 1.1 constant_dynamic-slice_fusion.7
  353.8 0.4 fusion.54
  355.0 1.2 constant_dynamic-update-slice_fusion.3
  356.2 1.1 constant_dynamic-slice_fusion.7
  358.5 1.2 constant_dynamic-update-slice_fusion.3
  359.7 1.4 copy.60
  361.1 0.7 reduce-scatter.6.cloned.1.call-update
  361.9 135.7 %reduce-scatter.10.cloned.1.call-done = f32[32,5]{1,0:T(8,128)} async-done(((f32[2048,5]{1,0:T(8,128)}), f32[32,5]{1,0:T(8,128)}) %reduce-scatter.10.cloned.1.call-update) | async-done | bytes 656 | tf_op jit(solution)/shard_map/reduce_scatter | solution.py:99
  497.6 148.2 %reduce-scatter.6.cloned.1.call-done = f32[32,640]{1,0:T(8,128)} async-done(((f32[2048,640]{1,0:T(8,128)}), f32[32,640]{1,0:T(8,128)}) %reduce-scatter.6.cloned.1.call-update) | async-done | bytes 81936 | tf_op jit(solution)/shard_map/reduce_scatter | solution.py:98
  645.8 0.8 div.11
  646.6 4.8 convolution_convert_fusion
  651.5 24.8 %reduce-scatter.8.cloned.1.call-done = bf16[32,1280]{1,0:T(8,128)(2,1)} async-done(((bf16[32,5120]{1,0:T(8,128)(2,1)}), bf16[32,1280]{1,0:T(8,128)(2,1)}) %reduce-scatter.8.cloned.1.call-update) | async-done | bytes 81936 | tf_op jit(solution)/shard_map/reduce_scatter | solution.py:103
  676.2 1.6 multiply_convert_fusion
  (44 shorter events, 5.4 us)
Async XLA Ops:
  6.5 2.2 copy-start
  6.5 85.5 %all-gather.2.cloned.1.call-start = ((), (), s32[]{:S(2)}) async-start(), calls=%async_computation.3 | async-start | bytes 2662400 | tf_op jit(solution)/shard_map/all_gather | solution.py:93
  7.3 490.3 %reduce-scatter.10.cloned.1.call-start = ((), (), s32[]{:S(2)}) async-start(), calls=%async_computation.6 | async-start | bytes 1064960 | tf_op jit(solution)/shard_map/reduce_scatter | solution.py:99
  361.1 284.7 %reduce-scatter.6.cloned.1.call-start = ((), (), s32[]{:S(2)}) async-start(), calls=%async_computation.4 | async-start | bytes 5324800 | tf_op jit(solution)/shard_map/reduce_scatter | solution.py:98
  361.8 314.4 %reduce-scatter.8.cloned.1.call-start = ((), (), s32[]{:S(2)}) async-start(), calls=%async_computation.5 | async-start | bytes 409600 | tf_op jit(solution)/shard_map/reduce_scatter | solution.py:103
  646.6 29.7 %copy-start.1 = (f32[1280]{0:T(1024)S(1)}, f32[1280]{0:T(1024)}, u32[]{:S(2)}) copy-start(f32[1280]{0:T(1024)} %param.19) | copy-start | bytes 15364
Sparse Core Ops, SparseCore 0:
  10.1 81.9 all-gather.1
  361.2 136.3 reduce-scatter.9
  501.7 143.9 reduce-scatter.5
  651.6 24.6 reduce-scatter.7
where the time goes:
time: 686 us; the launch traced here: 684 us
  waiting for transfers between devices  390 us (57%)
  blocking collectives  243 us (35%)
  local copies, waits for them, and re-layouts  22.5 us (3%)
  between operations  13.9 us (2%)
  matrix products  11.7 us (2%)
    pmax x1, blocking collectives, on_device(): lax.pmax(row_tops.astype(jnp.bfloat16), 'seq').astype(row_tops.dtype)  243 us
    reduce_scatter x1, waiting for transfers between devices, on_device(): lax.psum_scatter(summed, 'seq', scatter_dimension=0, tiled=True)  148 us
    reduce_scatter x1, waiting for transfers between devices, on_device(): lax.psum_scatter(totals, 'seq', scatter_dimension=0, tiled=True)  136 us
    all_gather x1, waiting for transfers between devices, on_device(): rows_all = lax.all_gather(queries, 'seq', axis=0, tiled=True)  80.3 us
    reduce_scatter x1, waiting for transfers between devices, on_device(): lax.psum_scatter(partial_rows.astype(jnp.bfloat16), 'head', scatter_dimen...  24.8 us
  transfers between devices with their start and end apart: 4, of which 4 were waited for; matrix products, arithmetic and copies ran while one was open for 1% of the time, Pallas kernels for 0%

commit v1 on v0

v1 whole, which is shorter than its diff:
```python
import functools
import math

import jax
import jax.numpy as jnp
from jax import lax
from jax.experimental import pallas as pl
from jax.experimental.pallas import tpu as pltpu
from jax.sharding import PartitionSpec as P

HD = 128
X = 4
CORES = 2
MESH = pl.DeviceIdType.MESH


def kernel(
    rings,
    q_hbm,
    new_k_hbm,
    new_v_hbm,
    cache_k_hbm,
    cache_v_hbm,
    weight_hbm,
    gate_ref,
    index_ref,
    count_ref,
    out_ref,
    cache,
    fresh,
    q_buf,
    kv_buf,
    o_send,
    o_recv,
    stat_send,
    stat_recv,
    weight,
    proj,
    y_send,
    y_recv,
    local_sem,
    q_ssem,
    q_rsem,
    own_ssem,
    own_rsem,
    relay_ssem,
    relay_rsem,
    pair_ssem,
    pair_rsem,
    o_ssem,
    o_rsem,
    stat_ssem,
    stat_rsem,
    y_ssem,
    y_rsem,
):
    depth, width = rings
    heads = q_buf.shape[0]
    slots = q_buf.shape[2]
    tokens = kv_buf.shape[3]
    out_cols = out_ref.shape[1]
    groups = stat_send.shape[1]
    per_group = depth // groups
    factor = HD ** (-0.5) * math.log2(math.e)

    me = lax.axis_index("seq")
    y = lax.axis_index("head")
    z = me // (X * CORES)
    x = (me // CORES) % X
    core = me % CORES

    def at_seq(z_at, x_at, core_at):
        return {"seq": (z_at * X + x_at) * CORES + core_at, "head": y}

    def z_peer(step):
        return at_seq((z + step) % depth, x, core)

    def y_peer(step):
        return {"seq": me, "head": (y + step) % width}

    right = at_seq(z, (x + 1) % X, core)
    left = at_seq(z, (x + X - 1) % X, core)
    sibling = at_seq(z, x, 1 - core)

    def remote(src, dst, send, recv, device):
        return pltpu.make_async_remote_copy(
            src_ref=src,
            dst_ref=dst,
            send_sem=send,
            recv_sem=recv,
            device_id=device,
            device_id_type=MESH,
        )

    barrier = pltpu.get_barrier_semaphore()
    peers = (
        [z_peer(step) for step in range(1, depth)]
        + [y_peer(step) for step in range(1, width)]
        + [right, left, sibling]
    )
    for peer in peers:
        pl.semaphore_signal(barrier, inc=1, device_id=peer, device_id_type=MESH)

    loads = [
        pltpu.make_async_copy(cache_k_hbm, cache.at[0], local_sem.at[0]),
        pltpu.make_async_copy(cache_v_hbm, cache.at[1], local_sem.at[1]),
        pltpu.make_async_copy(new_k_hbm, fresh.at[0], local_sem.at[2]),
        pltpu.make_async_copy(new_v_hbm, fresh.at[1], local_sem.at[3]),
    ]
    q_loads = [
        pltpu.make_async_copy(
            q_hbm.at[:, pl.ds(h * HD, HD)], q_buf.at[h, 0], local_sem.at[5 + h]
        )
        for h in range(heads)
    ]
    weight_load = pltpu.make_async_copy(weight_hbm, weight, local_sem.at[4])
    for load in loads + q_loads + [weight_load]:
        load.start()

    matches = (
        lax.broadcasted_iota(jnp.int32, (tokens, slots), 0) == index_ref[...]
    ) & (lax.broadcasted_iota(jnp.int32, (tokens, slots), 1) < count_ref[...])
    chosen = matches.astype(jnp.float32)
    replaced = jnp.max(chosen, axis=1, keepdims=True) > 0.5
    chosen = chosen.astype(jnp.bfloat16)
    for load in loads:
        load.wait()
    for part in range(2):
        placed = jnp.dot(chosen, fresh[part], preferred_element_type=jnp.float32)
        for h in range(heads):
            cols = slice(h * HD, (h + 1) * HD)
            kv_buf[h, part, 0] = jnp.where(
                replaced, placed[:, cols], cache[part, :, cols].astype(jnp.float32)
            ).astype(jnp.bfloat16)
    for load in q_loads:
        load.wait()

    pl.semaphore_wait(barrier, len(peers))

    def own_copies(h):
        src = kv_buf.at[h, :, 0]
        return (
            remote(src, kv_buf.at[h, :, 1], own_ssem.at[h, 0], own_rsem.at[h, 0], right),
            remote(src, kv_buf.at[h, :, 2], own_ssem.at[h, 1], own_rsem.at[h, 1], left),
        )

    def relay_copies(h):
        return (
            remote(
                kv_buf.at[h, 0, 1], kv_buf.at[h, 0, 3], relay_ssem.at[h, 0], relay_rsem.at[h, 0], right
            ),
            remote(
                kv_buf.at[h, 1, 2], kv_buf.at[h, 1, 3], relay_ssem.at[h, 1], relay_rsem.at[h, 1], left
            ),
        )

    def pair_copy(h, which):
        first, count = ((0, 1), (1, 2), (3, 1))[which]
        return remote(
            kv_buf.at[h, :, pl.ds(first, count)],
            kv_buf.at[h, :, pl.ds(X + first, count)],
            pair_ssem.at[h, which],
            pair_rsem.at[h, which],
            sibling,
        )

    def q_copy(h, step):
        return remote(
            q_buf.at[h, 0], q_buf.at[h, step], q_ssem.at[h, step], q_rsem.at[h, step], z_peer(step)
        )

    def o_copy(h, step):
        return remote(
            o_send.at[h, step],
            o_recv.at[h, step],
            o_ssem.at[h, step],
            o_rsem.at[h, step],
            z_peer(depth - step),
        )

    def stat_copy(h, step):
        return remote(
            stat_send.at[h, step // per_group],
            stat_recv.at[h, step],
            stat_ssem.at[h, step],
            stat_rsem.at[h, step],
            z_peer(depth - step),
        )

    far_first = sorted(range(1, depth), key=lambda step: -min(step, depth - step))

    def each_head(body):
        lax.fori_loop(0, heads, lambda h, carry: (body(h), carry)[1], 0)

    for h in range(min(2, heads)):
        for copy in own_copies(h):
            copy.start()
        pair_copy(h, 0).start()

    def send_queries(h):
        for step in far_first:
            q_copy(h, step).start()

    each_head(send_queries)

    lane = lax.broadcasted_iota(jnp.int32, (per_group * slots, HD), 1)
    row = lax.broadcasted_iota(jnp.int32, (per_group * slots, HD), 0)
    diagonal = lane == row

    def to_row(column):
        spread = jnp.broadcast_to(column, (per_group * slots, HD))
        return jnp.sum(jnp.where(diagonal, spread, 0.0), axis=0, keepdims=True)

    def attend(h):
        queries = q_buf[h].reshape(depth * slots, HD)
        keys = kv_buf[h, 0].reshape(X * CORES * tokens, HD)
        values = kv_buf[h, 1].reshape(X * CORES * tokens, HD)
        scores = (
            lax.dot_general(
                queries, keys, (((1,), (1,)), ((), ())), preferred_element_type=jnp.float32
            )
            * factor
        )
        top = jnp.max(scores, axis=1, keepdims=True)
        weights = jnp.exp2(scores - top)
        total = jnp.sum(weights, axis=1, keepdims=True)
        summed = jnp.dot(
            weights.astype(jnp.bfloat16), values, preferred_element_type=jnp.float32
        ).astype(jnp.bfloat16)
        o_send[h] = summed.reshape(depth, slots, HD)
        o_recv[h, 0] = summed[:slots]
        for g in range(groups):
            rows = slice(g * per_group * slots, (g + 1) * per_group * slots)
            top_row, total_row = to_row(top[rows]), to_row(total[rows])
            stat_send[h, g, 0] = top_row
            stat_send[h, g, 1] = total_row
            if g == 0:
                stat_recv[h, 0, 0] = top_row
                stat_recv[h, 0, 1] = total_row

    def stage(step, carry):
        @pl.when(step < heads)
        def _():
            for copy in own_copies(step):
                copy.wait_recv()
            for copy in relay_copies(step):
                copy.start()
            pair_copy(step, 1).start()

            @pl.when(step + 2 < heads)
            def _():
                for copy in own_copies(step + 2):
                    copy.start()
                pair_copy(step + 2, 0).start()

        @pl.when(step >= 1)
        def _():
            h = step - 1
            for copy in relay_copies(h):
                copy.wait_recv()
            pair_copy(h, 2).start()
            for ring in range(1, depth):
                q_copy(h, ring).wait_recv()
            for which in range(3):
                pair_copy(h, which).wait_recv()
            attend(h)
            for ring in far_first:
                o_copy(h, ring).start()
                stat_copy(h, ring).start()

        return carry

    lax.fori_loop(0, heads + 1, stage, 0)

    weight_load.wait()
    lane_row = lax.broadcasted_iota(jnp.int32, (1, HD), 1) // slots
    lanes = depth * slots
    spot = lax.broadcasted_iota(jnp.int32, (slots, lanes), 1) % slots
    on_row = spot == lax.broadcasted_iota(jnp.int32, (slots, lanes), 0)

    def over_lanes(rows, op):
        folded = functools.reduce(op, rows)
        shift = slots
        while shift < HD:
            folded = op(folded, pltpu.roll(folded, shift, 1))
            shift *= 2
        return folded

    def combined(h):
        for step in range(1, depth):
            o_copy(h, step).wait_recv()
            stat_copy(h, step).wait_recv()
        tops, totals = [], []
        for g in range(groups):
            top_row, total_row = (stat_recv[h, g * per_group, 0], stat_recv[h, g * per_group, 1])
            for k in range(1, per_group):
                here = lane_row == k
                top_row = jnp.where(here, stat_recv[h, g * per_group + k, 0], top_row)
                total_row = jnp.where(here, stat_recv[h, g * per_group + k, 1], total_row)
            tops.append(top_row)
            totals.append(total_row)
        peak = over_lanes(tops, jnp.maximum)
        shares = [jnp.exp2(top_row - peak) for top_row in tops]
        whole = over_lanes([share * total for share, total in zip(shares, totals)], jnp.add)
        factors = jnp.concatenate([share / whole for share in shares], axis=1)
        spread = jnp.where(on_row, jnp.broadcast_to(factors, (slots, lanes)), 0.0)
        high = spread.astype(jnp.bfloat16)
        low = (spread - high.astype(jnp.float32)).astype(jnp.bfloat16)
        parts = o_recv[h].reshape(lanes, HD)
        return (
            jnp.dot(high, parts, preferred_element_type=jnp.float32)
            + jnp.dot(low, parts, preferred_element_type=jnp.float32)
        ).astype(jnp.bfloat16)

    def projected(attended, h, step):
        start = pl.multiple_of(((y + step) % width) * out_cols, HD)
        block = weight[pl.ds(pl.multiple_of(h * HD, HD), HD), pl.ds(start, out_cols)]
        return jnp.dot(attended, block, preferred_element_type=jnp.float32)

    proj[...] = jnp.zeros_like(proj)

    def project(h, carry):
        attended = combined(h)
        for step in range(width):
            proj[step] += projected(attended, h, step)
        return carry

    lax.fori_loop(0, heads - 1, project, 0)

    def y_copy(step):
        return remote(
            y_send.at[step - 1], y_recv.at[step - 1], y_ssem.at[step - 1], y_rsem.at[step - 1], y_peer(step)
        )

    attended = combined(heads - 1)
    for step in sorted(range(1, width), key=lambda step: -min(step, width - step)):
        y_send[step - 1] = (proj[step] + projected(attended, heads - 1, step)).astype(jnp.bfloat16)
        y_copy(step).start()
    result = proj[0] + projected(attended, heads - 1, 0)
    for step in range(1, width):
        y_copy(step).wait_recv()
        result += y_recv[step - 1].astype(jnp.float32)
    live = lax.broadcasted_iota(jnp.int32, (slots, out_cols), 0) < count_ref[...]
    out_ref[...] = (
        gate_ref[...] * result * live.astype(jnp.float32)
    ).astype(jnp.bfloat16)

    def drain(h):
        for copy in own_copies(h) + relay_copies(h):
            copy.wait_send()
        for which in range(3):
            pair_copy(h, which).wait_send()
        for step in range(1, depth):
            q_copy(h, step).wait_send()
            o_copy(h, step).wait_send()
            stat_copy(h, step).wait_send()

    each_head(drain)
    for step in range(1, width):
        y_copy(step).wait_send()


def on_device(
    depth,
    width,
    queries,
    new_keys,
    new_values,
    key_cache,
    value_cache,
    out_weight,
    gate,
    refresh_index,
    refresh_count,
):
    slots, row_width = queries.shape
    tokens = key_cache.shape[0]
    heads = row_width // HD
    out_cols = gate.shape[0]
    groups = max(1, depth * slots // HD)
    bf16, f32 = jnp.bfloat16, jnp.float32
    dma = pltpu.SemaphoreType.DMA
    any_spec = pl.BlockSpec(memory_space=pl.ANY)
    vmem_spec = pl.BlockSpec(memory_space=pltpu.VMEM)
    return pl.pallas_call(
        functools.partial(kernel, (depth, width)),
        out_shape=jax.ShapeDtypeStruct((slots, out_cols), bf16),
        in_specs=[any_spec] * 6 + [vmem_spec] * 3,
        out_specs=vmem_spec,
        scratch_shapes=[
            pltpu.VMEM((2, tokens, row_width), bf16),
            pltpu.VMEM((2, slots, row_width), bf16),
            pltpu.VMEM((heads, depth, slots, HD), bf16),
            pltpu.VMEM((heads, 2, X * CORES, tokens, HD), bf16),
            pltpu.VMEM((heads, depth, slots, HD), bf16),
            pltpu.VMEM((heads, depth, slots, HD), bf16),
            pltpu.VMEM((heads, groups, 2, 1, HD), f32),
            pltpu.VMEM((heads, depth, 2, 1, HD), f32),
            pltpu.VMEM(out_weight.shape, bf16),
            pltpu.VMEM((width, slots, out_cols), f32),
            pltpu.VMEM((max(1, width - 1), slots, out_cols), bf16),
            pltpu.VMEM((max(1, width - 1), slots, out_cols), bf16),
            dma((5 + heads,)),
            dma((heads, depth)),
            dma((heads, depth)),
            dma((heads, 2)),
            dma((heads, 2)),
            dma((heads, 2)),
            dma((heads, 2)),
            dma((heads, 3)),
            dma((heads, 3)),
            dma((heads, depth)),
            dma((heads, depth)),
            dma((heads, depth)),
            dma((heads, depth)),
            dma((max(1, width - 1),)),
            dma((max(1, width - 1),)),
        ],
        compiler_params=pltpu.CompilerParams(
            collective_id=0, has_side_effects=True, vmem_limit_bytes=40 << 20
        ),
    )(
        queries,
        new_keys,
        new_values,
        key_cache,
        value_cache,
        out_weight,
        gate.reshape(1, -1),
        refresh_index,
        refresh_count.reshape(1, 1),
    )


def solution(mesh):
    depth = mesh.shape["seq"] // (X * CORES)
    width = mesh.shape["head"]
    return jax.shard_map(
        functools.partial(on_device, depth, width),
        mesh=mesh,
        in_specs=(
            P("seq", "head"),
            P("seq", "head"),
            P("seq", "head"),
            P("seq", "head"),
            P("seq", "head"),
            P("head", None),
            P("head"),
            P("seq", None),
            P("seq"),
        ),
        out_specs=P("seq", "head"),
        check_vma=False,
    )
```

time: 686 us -> 53.9 us (0.08)
  waiting for transfers between devices: 390 us -> 0 us
  blocking collectives: 243 us -> 0 us
  Pallas kernels: 0 us -> 43.9 us
  local copies, waits for them, and re-layouts: 22.5 us -> 9.02 us
  between operations: 13.9 us -> 0.67 us
  matrix products: 11.7 us -> 0 us
    reduce_scatter x3 -> x0, waiting for transfers between devices: 309 us -> none  [the longest x1 148 us: on_device(): lax.psum_scatter(summed, 'seq', scatter_dimension=0, tiled=True)]
    pmax x1 -> x0, blocking collectives: 243 us -> none  [on_device(): lax.pmax(row_tops.astype(jnp.bfloat16), 'seq').astype(row_tops.dtype)]
    all_gather x1 -> x0, waiting for transfers between devices: 80.3 us -> none  [on_device(): rows_all = lax.all_gather(queries, 'seq', axis=0, tiled=True)]
    pallas_call x0 -> x1, Pallas kernels: none -> 43.9 us  [on_device(): pl.pallas_call(functools.partial(kernel, (depth, width)), out_shape=jax.S...]
    dot_general x15 -> x0, matrix products: 11.7 us -> none  [the longest x1 4.84 us: on_device(): jnp.dot(attended, out_weight, preferred_element_type=jnp.float32)]
    dynamic_slice x8 -> x0, local copies, waits for them, and re-layouts: 9.06 us -> none  [local_top(): lax.map(lambda q_block: jnp.max(score_block(q_block, keys_heads, key_scal...]
    unnamed x5 -> x15, local copies, waits for them, and re-layouts: 1.4 us -> 8.32 us
  transfers between devices with their start and end apart: 4 -> 0, of which waited for: 4 -> 0; matrix products, arithmetic and copies ran while one was open for 1% -> 0% of each run, Pallas kernels for 0% -> 0%
where the time goes in v1:
time: 53.9 us; the launch traced here: 53.5 us
  Pallas kernels  43.9 us (81%)
  local copies, waits for them, and re-layouts  9.02 us (17%)
  between operations  0.67 us (1%)
    pallas_call x1, Pallas kernels, on_device(): pl.pallas_call(functools.partial(kernel, (depth, width)), out_shape=jax.S...  43.9 us
    unnamed x15, local copies, waits for them, and re-layouts  8.32 us

profile of v1, /device:TPU:1, one launch (start us, length us, event | category | flops | bytes accessed | tf_op | source)
XLA Modules:
  0.0 53.5 jit_solution(8376198390413347936)
XLA Ops:
  0.7 0.7 %reshape.6.gate_ref = f32[1,1280]{1,0:T(1,128)S(1)} reshape(f32[1280]{0:T(1024)} %param.15) | data formatting | bytes 10240 | tf_op jit(solution)/shard_map/reshape | solution.py:429
  1.4 0.0 copy-start
  1.4 2.9 %copy-done = bf16[640,5120]{1,0:T(8,128)(2,1)S(1)} copy-done((bf16[640,5120]{1,0:T(8,128)(2,1)S(1)}, bf16[640,5120]{1,0:T(8,128)(2,1)}, u32[]{:S(2)}) %copy-start) | copy-done | bytes 6553624
  4.2 0.0 copy-start.1
  4.2 0.9 %copy-done.1 = bf16[128,640]{1,0:T(8,128)(2,1)S(1)} copy-done((bf16[128,640]{1,0:T(8,128)(2,1)S(1)}, bf16[128,640]{1,0:T(8,128)(2,1)}, u32[]{:S(2)}) %copy-start.1) | copy-done | bytes 163864
  5.1 0.0 copy-start.2
  5.1 0.9 %copy-done.2 = bf16[128,640]{1,0:T(8,128)(2,1)S(1)} copy-done((bf16[128,640]{1,0:T(8,128)(2,1)S(1)}, bf16[128,640]{1,0:T(8,128)(2,1)}, u32[]{:S(2)}) %copy-start.2) | copy-done | bytes 163864
  6.0 0.0 copy-start.3
  6.0 0.8 %copy-done.3 = bf16[32,640]{1,0:T(8,128)(2,1)S(1)} copy-done((bf16[32,640]{1,0:T(8,128)(2,1)S(1)}, bf16[32,640]{1,0:T(8,128)(2,1)}, u32[]{:S(2)}) %copy-start.3) | copy-done | bytes 40984
  6.8 0.0 copy-start.4
  6.8 0.8 %copy-done.4 = bf16[32,640]{1,0:T(8,128)(2,1)S(1)} copy-done((bf16[32,640]{1,0:T(8,128)(2,1)S(1)}, bf16[32,640]{1,0:T(8,128)(2,1)}, u32[]{:S(2)}) %copy-start.4) | copy-done | bytes 40984
  7.6 0.0 copy-start.5
  7.6 0.8 %copy-done.5 = bf16[32,640]{1,0:T(8,128)(2,1)S(1)} copy-done((bf16[32,640]{1,0:T(8,128)(2,1)S(1)}, bf16[32,640]{1,0:T(8,128)(2,1)}, u32[]{:S(2)}) %copy-start.5) | copy-done | bytes 40984
  8.4 0.0 copy-start.6
  8.4 0.7 %copy-done.6 = s32[1,32]{1,0:T(1,128)S(1)} copy-done((s32[1,32]{1,0:T(1,128)S(1)}, s32[1,32]{1,0:T(1,128)}, u32[]{:S(2)}) %copy-start.6) | copy-done | bytes 152
  9.0 43.9 %shard_map.91 = bf16[32,1280]{1,0:T(8,128)(2,1)S(1)} custom-call(bf16[32,640]{1,0:T(8,128)(2,1)S(1)} %copy-done.3, bf16[32,640]{1,0:T(8,128)(2,1)S(1)} %copy-done.4, bf16[32,640]{1,0:T(8,128)(2,1)S(1)} %copy-done.5, bf16[128,640]{1,0:T(8,128)(2,1)S(1)} %copy-done.1, bf16[128,640]{1,0:T(8,128)(2,1)S(1)} %copy-done.2, bf16[640,5120]{1,0:T(8,128)(2,1)S(1)} %copy-done, ...), custom_call_target="tpu_custom_call" | custom-call | tf_op jit(solution)/shard_map/pallas_call | solution.py:385
  52.9 0.6 %copy.12 = bf16[32,1280]{1,0:T(8,128)(2,1)} copy(bf16[32,1280]{1,0:T(8,128)(2,1)S(1)} %shard_map.91) | data formatting | bytes 163840
Async XLA Ops:
  1.4 2.9 %copy-start = (bf16[640,5120]{1,0:T(8,128)(2,1)S(1)}, bf16[640,5120]{1,0:T(8,128)(2,1)}, u32[]{:S(2)}) copy-start(bf16[640,5120]{1,0:T(8,128)(2,1)} %weight_hbm.1) | copy-start | bytes 19660804
  4.2 0.9 %copy-start.1 = (bf16[128,640]{1,0:T(8,128)(2,1)S(1)}, bf16[128,640]{1,0:T(8,128)(2,1)}, u32[]{:S(2)}) copy-start(bf16[128,640]{1,0:T(8,128)(2,1)} %cache_k_hbm.1) | copy-start | bytes 491524
  5.1 0.9 %copy-start.2 = (bf16[128,640]{1,0:T(8,128)(2,1)S(1)}, bf16[128,640]{1,0:T(8,128)(2,1)}, u32[]{:S(2)}) copy-start(bf16[128,640]{1,0:T(8,128)(2,1)} %cache_v_hbm.1) | copy-start | bytes 491524
  6.0 0.8 %copy-start.3 = (bf16[32,640]{1,0:T(8,128)(2,1)S(1)}, bf16[32,640]{1,0:T(8,128)(2,1)}, u32[]{:S(2)}) copy-start(bf16[32,640]{1,0:T(8,128)(2,1)} %q_hbm.1) | copy-start | bytes 122884
  6.8 0.8 %copy-start.4 = (bf16[32,640]{1,0:T(8,128)(2,1)S(1)}, bf16[32,640]{1,0:T(8,128)(2,1)}, u32[]{:S(2)}) copy-start(bf16[32,640]{1,0:T(8,128)(2,1)} %new_k_hbm.1) | copy-start | bytes 122884
  7.6 0.8 %copy-start.5 = (bf16[32,640]{1,0:T(8,128)(2,1)S(1)}, bf16[32,640]{1,0:T(8,128)(2,1)}, u32[]{:S(2)}) copy-start(bf16[32,640]{1,0:T(8,128)(2,1)} %new_v_hbm.1) | copy-start | bytes 122884
  8.4 0.7 %copy-start.6 = (s32[1,32]{1,0:T(1,128)S(1)}, s32[1,32]{1,0:T(1,128)}, u32[]{:S(2)}) copy-start(s32[1,32]{1,0:T(1,128)} %index_ref.1) | copy-start | bytes 388

commit v2 on v1

--- a/solution.py
+++ b/solution.py
@@ -12,6 +12,8 @@
 X = 4
 CORES = 2
 MESH = pl.DeviceIdType.MESH
+AHEAD = 3
+LAG = 2
 
 
 def kernel(
@@ -22,7 +24,6 @@
     cache_k_hbm,
     cache_v_hbm,
     weight_hbm,
-    gate_ref,
     index_ref,
     count_ref,
     out_ref,
@@ -192,7 +193,7 @@
     def each_head(body):
         lax.fori_loop(0, heads, lambda h, carry: (body(h), carry)[1], 0)
 
-    for h in range(min(2, heads)):
+    for h in range(min(AHEAD, heads)):
         for copy in own_copies(h):
             copy.start()
         pair_copy(h, 0).start()
@@ -247,18 +248,22 @@
                 copy.start()
             pair_copy(step, 1).start()
 
-            @pl.when(step + 2 < heads)
+            @pl.when(step + AHEAD < heads)
             def _():
-                for copy in own_copies(step + 2):
+                for copy in own_copies(step + AHEAD):
                     copy.start()
-                pair_copy(step + 2, 0).start()
-
-        @pl.when(step >= 1)
+                pair_copy(step + AHEAD, 0).start()
+
+        @pl.when((step >= 1) & (step <= heads))
         def _():
             h = step - 1
             for copy in relay_copies(h):
                 copy.wait_recv()
             pair_copy(h, 2).start()
+
+        @pl.when(step >= LAG)
+        def _():
+            h = step - LAG
             for ring in range(1, depth):
                 q_copy(h, ring).wait_recv()
             for which in range(3):
@@ -270,7 +275,7 @@
 
         return carry
 
-    lax.fori_loop(0, heads + 1, stage, 0)
+    lax.fori_loop(0, heads + LAG, stage, 0)
 
     weight_load.wait()
     lane_row = lax.broadcasted_iota(jnp.int32, (1, HD), 1) // slots
@@ -340,10 +345,7 @@
     for step in range(1, width):
         y_copy(step).wait_recv()
         result += y_recv[step - 1].astype(jnp.float32)
-    live = lax.broadcasted_iota(jnp.int32, (slots, out_cols), 0) < count_ref[...]
-    out_ref[...] = (
-        gate_ref[...] * result * live.astype(jnp.float32)
-    ).astype(jnp.bfloat16)
+    out_ref[...] = result
 
     def drain(h):
         for copy in own_copies(h) + relay_copies(h):
@@ -382,10 +384,10 @@
     dma = pltpu.SemaphoreType.DMA
     any_spec = pl.BlockSpec(memory_space=pl.ANY)
     vmem_spec = pl.BlockSpec(memory_space=pltpu.VMEM)
-    return pl.pallas_call(
+    projected = pl.pallas_call(
         functools.partial(kernel, (depth, width)),
-        out_shape=jax.ShapeDtypeStruct((slots, out_cols), bf16),
-        in_specs=[any_spec] * 6 + [vmem_spec] * 3,
+        out_shape=jax.ShapeDtypeStruct((slots, out_cols), f32),
+        in_specs=[any_spec] * 6 + [vmem_spec] * 2,
         out_specs=vmem_spec,
         scratch_shapes=[
             pltpu.VMEM((2, tokens, row_width), bf16),
@@ -417,7 +419,7 @@
             dma((max(1, width - 1),)),
         ],
         compiler_params=pltpu.CompilerParams(
-            collective_id=0, has_side_effects=True, vmem_limit_bytes=40 << 20
+            collective_id=0, has_side_effects=True, vmem_limit_bytes=67_043_328
         ),
     )(
         queries,
@@ -426,10 +428,11 @@
         key_cache,
         value_cache,
         out_weight,
-        gate.reshape(1, -1),
         refresh_index,
         refresh_count.reshape(1, 1),
     )
+    live = lax.broadcasted_iota(jnp.int32, (slots, out_cols), 0) < refresh_count[0]
+    return (gate[None] * jnp.where(live, projected, 0.0)).astype(bf16)
 
 
 def solution(mesh):

time: 53.9 us -> 46.7 us (0.87)
  local copies, waits for them, and re-layouts: 9.02 us -> 0 us
  other arithmetic: 0 us -> 2.22 us
    unnamed x15 -> x0, local copies, waits for them, and re-layouts: 8.32 us -> none
    convert_element_type x0 -> x1, other arithmetic: none -> 1.66 us  [on_device(): return (gate[None] * jnp.where(live, projected, 0.0)).astype(bf16)]
    reshape x1 -> x0, local copies, waits for them, and re-layouts: 0.7 us -> none  [on_device(): gate.reshape(1, -1)]
    lt x0 -> x1, other arithmetic: none -> 0.57 us  [on_device(): lax.broadcasted_iota(jnp.int32, (slots, out_cols), 0) < refresh_count[0]]
where the time goes in v2:
time: 46.7 us; the launch traced here: 46.6 us
  Pallas kernels  43.7 us (94%)
  other arithmetic  2.22 us (5%)
  between operations  0.66 us (1%)
    pallas_call x1, Pallas kernels, on_device(): pl.pallas_call(functools.partial(kernel, (depth, width)), out_shape=jax.S...  43.7 us
    convert_element_type x1, other arithmetic, on_device(): return (gate[None] * jnp.where(live, projected, 0.0)).astype(bf16)  1.66 us

profile of v2, /device:TPU:1, one launch (start us, length us, event | category | flops | bytes accessed | tf_op | source)
XLA Modules:
  0.0 46.6 jit_solution(14904855212502129791)
XLA Ops:
  0.7 0.6 %iota_compare_fusion = pred[32]{0:T(512)(128)(4,1)} fusion(s32[]{:T(128)} %bitcast.2), kind=kLoop, calls=%fused_computation.1 | loop fusion | flops 32 | bytes 36 | tf_op jit(solution)/shard_map/lt | solution.py:434
  1.2 43.7 %shard_map.91 = f32[32,1280]{1,0:T(8,128)} custom-call(bf16[32,640]{1,0:T(8,128)(2,1)} %q_hbm.1, bf16[32,640]{1,0:T(8,128)(2,1)} %new_k_hbm.1, bf16[32,640]{1,0:T(8,128)(2,1)} %new_v_hbm.1, bf16[128,640]{1,0:T(8,128)(2,1)} %cache_k_hbm.1, bf16[128,640]{1,0:T(8,128)(2,1)} %cache_v_hbm.1, bf16[640,5120]{1,0:T(8,128)(2,1)} %weight_hbm.1, s32[1,32]{1,0:T(1,128)} %index_ref.1, ...), custom_call_target="tpu_custom_call" | custom-call | tf_op jit(solution)/shard_map/pallas_call | solution.py:387
  44.9 1.7 %multiply_convert_fusion = bf16[32,1280]{1,0:T(8,128)(2,1)} fusion(f32[32,1280]{1,0:T(8,128)} %shard_map.91, f32[1280]{0:T(1024)} %param.15, pred[32]{0:T(512)(128)(4,1)} %iota_compare_fusion), kind=kLoop, calls=%fused_computation | loop fusion | flops 122880 | bytes 250912 | tf_op jit(solution)/shard_map/convert_element_type | solution.py:435

commit v3 on v2

--- a/solution.py
+++ b/solution.py
@@ -54,6 +54,8 @@
     stat_rsem,
     y_ssem,
     y_rsem,
+    z_near,
+    y_near,
 ):
     depth, width = rings
     heads = q_buf.shape[0]
@@ -95,8 +97,7 @@
 
     barrier = pltpu.get_barrier_semaphore()
     peers = (
-        [z_peer(step) for step in range(1, depth)]
-        + [y_peer(step) for step in range(1, width)]
+        [z_peer(1), z_peer(depth - 1), y_peer(1), y_peer(width - 1)]
         + [right, left, sibling]
     )
     for peer in peers:
@@ -198,11 +199,23 @@
             copy.start()
         pair_copy(h, 0).start()
 
-    def send_queries(h):
-        for step in far_first:
+    def send_queries(distance, h):
+        for step in sorted({distance, depth - distance}):
             q_copy(h, step).start()
 
-    each_head(send_queries)
+    def announce(sem, peer):
+        pl.semaphore_signal(sem, inc=1, device_id=peer, device_id_type=MESH)
+
+    announce(y_near, y_peer(1))
+    for distance in range(1, depth // 2 + 1):
+        if distance > 1:
+            pl.semaphore_wait(z_near.at[0, distance - 1], 1)
+            pl.semaphore_wait(z_near.at[1, distance - 1], 1)
+        if distance < depth // 2:
+            announce(z_near.at[0, distance], z_peer(1))
+            announce(z_near.at[1, distance], z_peer(depth - 1))
+        each_head(functools.partial(send_queries, distance))
+    pl.semaphore_wait(y_near, 1)
 
     lane = lax.broadcasted_iota(jnp.int32, (per_group * slots, HD), 1)
     row = lax.broadcasted_iota(jnp.int32, (per_group * slots, HD), 0)
@@ -417,6 +430,8 @@
             dma((heads, depth)),
             dma((max(1, width - 1),)),
             dma((max(1, width - 1),)),
+            pltpu.SemaphoreType.REGULAR((2, max(2, depth // 2))),
+            pltpu.SemaphoreType.REGULAR,
         ],
         compiler_params=pltpu.CompilerParams(
             collective_id=0, has_side_effects=True, vmem_limit_bytes=67_043_328

time: 46.7 us -> 46 us (0.985)
  Pallas kernels: 43.7 us -> 43 us
    pallas_call x1, Pallas kernels: 43.7 us -> 43 us  [on_device(): pl.pallas_call(functools.partial(kernel, (depth, width)), out_shape=jax.S...]
where the time goes in v3:
time: 46 us; the launch traced here: 45.9 us
  Pallas kernels  43 us (93%)
  other arithmetic  2.22 us (5%)
  between operations  0.66 us (1%)
    pallas_call x1, Pallas kernels, on_device(): pl.pallas_call(functools.partial(kernel, (depth, width)), out_shape=jax.S...  43 us
    convert_element_type x1, other arithmetic, on_device(): return (gate[None] * jnp.where(live, projected, 0.0)).astype(bf16)  1.66 us

profile of v3, /device:TPU:1, one launch (start us, length us, event | category | flops | bytes accessed | tf_op | source)
XLA Modules:
  0.0 45.9 jit_solution(622385077159280700)
XLA Ops:
  0.7 0.6 %iota_compare_fusion = pred[32]{0:T(512)(128)(4,1)} fusion(s32[]{:T(128)} %bitcast.2), kind=kLoop, calls=%fused_computation.1 | loop fusion | flops 32 | bytes 36 | tf_op jit(solution)/shard_map/lt | solution.py:449
  1.2 43.0 %shard_map.91 = f32[32,1280]{1,0:T(8,128)} custom-call(bf16[32,640]{1,0:T(8,128)(2,1)} %q_hbm.1, bf16[32,640]{1,0:T(8,128)(2,1)} %new_k_hbm.1, bf16[32,640]{1,0:T(8,128)(2,1)} %new_v_hbm.1, bf16[128,640]{1,0:T(8,128)(2,1)} %cache_k_hbm.1, bf16[128,640]{1,0:T(8,128)(2,1)} %cache_v_hbm.1, bf16[640,5120]{1,0:T(8,128)(2,1)} %weight_hbm.1, s32[1,32]{1,0:T(1,128)} %index_ref.1, ...), custom_call_target="tpu_custom_call" | custom-call | tf_op jit(solution)/shard_map/pallas_call | solution.py:400
  44.3 1.7 %multiply_convert_fusion = bf16[32,1280]{1,0:T(8,128)(2,1)} fusion(f32[32,1280]{1,0:T(8,128)} %shard_map.91, f32[1280]{0:T(1024)} %param.15, pred[32]{0:T(512)(128)(4,1)} %iota_compare_fusion), kind=kLoop, calls=%fused_computation | loop fusion | flops 122880 | bytes 250912 | tf_op jit(solution)/shard_map/convert_element_type | solution.py:450

commit v4 on v3

--- a/solution.py
+++ b/solution.py
@@ -116,7 +116,7 @@
         for h in range(heads)
     ]
     weight_load = pltpu.make_async_copy(weight_hbm, weight, local_sem.at[4])
-    for load in loads + q_loads + [weight_load]:
+    for load in loads + q_loads:
         load.start()
 
     matches = (
@@ -134,9 +134,6 @@
             kv_buf[h, part, 0] = jnp.where(
                 replaced, placed[:, cols], cache[part, :, cols].astype(jnp.float32)
             ).astype(jnp.bfloat16)
-    for load in q_loads:
-        load.wait()
-
     pl.semaphore_wait(barrier, len(peers))
 
     def own_copies(h):
@@ -198,6 +195,9 @@
         for copy in own_copies(h):
             copy.start()
         pair_copy(h, 0).start()
+    weight_load.start()
+    for load in q_loads:
+        load.wait()
 
     def send_queries(distance, h):
         for step in sorted({distance, depth - distance}):

time: 46 us -> 46 us (level)
  no operation moved by 1% of the time
where the time goes in v4:
time: 46 us; the launch traced here: 45.9 us
  Pallas kernels  43 us (93%)
  other arithmetic  2.22 us (5%)
  between operations  0.66 us (1%)
    pallas_call x1, Pallas kernels, on_device(): pl.pallas_call(functools.partial(kernel, (depth, width)), out_shape=jax.S...  43 us
    convert_element_type x1, other arithmetic, on_device(): return (gate[None] * jnp.where(live, projected, 0.0)).astype(bf16)  1.66 us

profile of v4, /device:TPU:1, one launch (start us, length us, event | category | flops | bytes accessed | tf_op | source)
XLA Modules:
  0.0 45.9 jit_solution(13508612734926740265)
XLA Ops:
  0.7 0.6 %iota_compare_fusion = pred[32]{0:T(512)(128)(4,1)} fusion(s32[]{:T(128)} %bitcast.2), kind=kLoop, calls=%fused_computation.1 | loop fusion | flops 32 | bytes 36 | tf_op jit(solution)/shard_map/lt | solution.py:449
  1.2 43.0 %shard_map.91 = f32[32,1280]{1,0:T(8,128)} custom-call(bf16[32,640]{1,0:T(8,128)(2,1)} %q_hbm.1, bf16[32,640]{1,0:T(8,128)(2,1)} %new_k_hbm.1, bf16[32,640]{1,0:T(8,128)(2,1)} %new_v_hbm.1, bf16[128,640]{1,0:T(8,128)(2,1)} %cache_k_hbm.1, bf16[128,640]{1,0:T(8,128)(2,1)} %cache_v_hbm.1, bf16[640,5120]{1,0:T(8,128)(2,1)} %weight_hbm.1, s32[1,32]{1,0:T(1,128)} %index_ref.1, ...), custom_call_target="tpu_custom_call" | custom-call | tf_op jit(solution)/shard_map/pallas_call | solution.py:400
  44.2 1.7 %multiply_convert_fusion = bf16[32,1280]{1,0:T(8,128)(2,1)} fusion(f32[32,1280]{1,0:T(8,128)} %shard_map.91, f32[1280]{0:T(1024)} %param.15, pred[32]{0:T(512)(128)(4,1)} %iota_compare_fusion), kind=kLoop, calls=%fused_computation | loop fusion | flops 122880 | bytes 250912 | tf_op jit(solution)/shard_map/convert_element_type | solution.py:450
